TPU v7x, 256 devices: a whole 4x4x8 slice. The times are simulated.
256 devices in a mesh: sector: 16 (over y, x_hi, core), depth: 16 (over x_lo, z).
Axes of the slice: x: 4 (x_hi: 2, x_lo: 2; x = x_hi * 2 + x_lo), y: 4, z: 8, core: 2. Of those that a mesh axis runs over, the one named last changes fastest.
Arguments:
- panel: bfloat16 [1048576, 128], P(('sector', 'depth')), may hold values from -6 to 6
- coords: int32 [3, 1048576], P(None, ('sector', 'depth')), may hold values from 0 to 127, as said below
- neighbours: int32 [8192, 32], P(('sector', 'depth')), may hold values from 0 to 8191, as said below
- ranges: float32 [3], replicated, may hold values from 6 to 20
Outputs:
- basis: float32 [1048576, 128], P(('sector', 'depth'))
- factor: float32 [128, 128], replicated
Inputs may be any that keep to these rules, and one draw needn't show every extreme that they name: `coords`: each device's 32 * 128 cells occupy every point of its own grid box exactly once: azimuth columns s * 8 to (s + 1) * 8 - 1 for sector s, radial rows 0 to 63, depth layers d * 8 to (d + 1) * 8 - 1 for slab d, in an arbitrary order; cell blocks are numbered sector-major, then slab, then block. `neighbours`: each row lists 32 different block columns, all of the row's depth slab and of sectors at most two away from its own around the cycle.
All inputs are finite; a program needn't handle non-finite values.
Results may differ from a plain program's by a relative error of at most 0.0065.
Values may be sent and summed in bfloat16 or wider, within the bound.
A program may use at most 128 MiB of HBM per device.

v0:
```python
import jax
import jax.numpy as jnp
from jax import lax
from jax.sharding import PartitionSpec as P

AZ_SEC = 8
CUTOFF = 3.0
NUGGET = 0.5


def passed_along(block, axis, distance):
    devices = range(lax.axis_size(axis))
    route = [((i - distance) % len(devices), i) for i in devices]
    return lax.ppermute(block, axis, route)


def as_sent(value):

    def short(part):
        return part.astype(jnp.bfloat16) if part.dtype == jnp.float32 else part

    return jax.tree.map(short, value)


def cov_blocks(home, remote, ranges, period):
    diffs = (home[:, None, :, :, None] - remote[:, :, :, None, :]).astype(jnp.float32)
    along = jnp.abs(diffs[:, :, 0])
    along = jnp.minimum(along, period - along)
    scaled = (
        (along / ranges[0]) ** 2
        + (diffs[:, :, 1] / ranges[1]) ** 2
        + (diffs[:, :, 2] / ranges[2]) ** 2
    )
    radius = jnp.sqrt(scaled)
    taper = jnp.maximum(1.0 - radius / CUTOFF, 0.0)
    weight = 8.0 / jnp.sqrt(jnp.float32(remote.shape[1] * remote.shape[3]))
    return (weight * jnp.exp(-radius) * taper * taper).astype(jnp.bfloat16)


def on_device(panel, coords, neighbours, ranges):
    block_count = neighbours.shape[0]
    block_size = panel.shape[0] // block_count
    width = panel.shape[1]
    sector_count = lax.axis_size("sector")
    slab_count = lax.axis_size("depth")
    my_sector = lax.axis_index("sector")
    blocked = panel.reshape(block_count, block_size, width)
    near_side = {}
    far_side = {}
    for direction in (1, -1):
        near_side[direction] = passed_along((blocked, coords), "sector", direction)
    for direction in (1, -1):
        far_side[direction] = passed_along(
            (near_side[direction][0], as_sent(near_side[direction][1])), "sector", direction
        )
    ordered = [far_side[1], near_side[1], (blocked, coords), near_side[-1], far_side[-1]]
    wide_panel = jnp.concatenate([member[0] for member in ordered], axis=0)
    wide_coords = jnp.concatenate(
        [member[1].reshape(3, block_count, block_size) for member in ordered], axis=1
    )
    wide_coords = jnp.transpose(wide_coords, (1, 0, 2))
    home_coords = jnp.transpose(coords.reshape(3, block_count, block_size), (1, 0, 2))
    column_sector = neighbours // (slab_count * block_count)
    step_away = (column_sector - my_sector + 2) % sector_count
    local_column = step_away * block_count + neighbours % block_count
    period = jnp.float32(AZ_SEC * sector_count)
    group = 4
    turns = block_count // group

    def one_group(inputs):
        rows_coords, rows_panel, rows_list = inputs
        kernel = cov_blocks(rows_coords, wide_coords[rows_list], ranges, period)
        product = jnp.einsum(
            "gnab,gnbc->gac", kernel, wide_panel[rows_list], preferred_element_type=jnp.float32
        )
        return product + NUGGET * rows_panel.astype(jnp.float32)

    image = lax.map(
        one_group,
        (
            home_coords.reshape(turns, group, 3, block_size),
            blocked.reshape(turns, group, block_size, width),
            local_column.reshape(turns, group, -1),
        ),
    )
    image = image.reshape(block_count * block_size, width)
    total_cells = jnp.float32(image.shape[0] * sector_count * slab_count)
    local_gram = (
        jnp.dot(image.T, image, precision=lax.Precision.HIGHEST, preferred_element_type=jnp.float32)
        / total_cells
    )
    lower = jnp.linalg.cholesky(lax.psum(local_gram, ("sector", "depth")))
    inverse = jax.scipy.linalg.solve_triangular(
        lower, jnp.eye(width, dtype=jnp.float32), lower=True
    )
    basis = jnp.dot(
        image, inverse.T, precision=lax.Precision.HIGHEST, preferred_element_type=jnp.float32
    )
    return (basis, lower.T)


def solution(mesh):
    in_specs = (
        P(("sector", "depth"), None),
        P(None, ("sector", "depth")),
        P(("sector", "depth"), None),
        P(),
    )
    out_specs = (P(("sector", "depth"), None), P())
    return jax.shard_map(
        on_device, mesh=mesh, in_specs=in_specs, out_specs=out_specs, check_vma=False
    )
```

profile of v0, /device:TPU:1, one launch (start us, length us, event | category | flops | bytes accessed | tf_op | source)
XLA Modules:
  0.0 625.7 jit_solution(4741672495982144289)
XLA Ops:
  15.9 15.5 %collective-permute-done = s32[3,4096]{1,0:T(4,128)S(1)} collective-permute-done((s32[3,4096]{1,0:T(4,128)}, s32[3,4096]{1,0:T(4,128)S(1)}, u32[]{:S(2)}, u32[]{:S(2)}) %collective-permute-start) | collective-permute-done | bytes 49184 | tf_op jit(solution)/shard_map/ppermute | solution.py:14
  41.3 5.5 collective-permute-start.7
  47.9 8.0 %collective-permute-done.5 = bf16[32,128,128]{2,1,0:T(8,128)(2,1)S(1)} collective-permute-done((bf16[32,128,128]{2,1,0:T(8,128)(2,1)}, bf16[32,128,128]{2,1,0:T(8,128)(2,1)S(1)}, u32[]{:S(2)}, u32[]{:S(2)}) %collective-permute-start.5) | collective-permute-done | bytes 1048608 | tf_op jit(solution)/shard_map/ppermute | solution.py:14
  59.0 9.7 %collective-permute-done.7 = bf16[32,128,128]{2,1,0:T(8,128)(2,1)S(1)} collective-permute-done((bf16[32,128,128]{2,1,0:T(8,128)(2,1)}, bf16[32,128,128]{2,1,0:T(8,128)(2,1)S(1)}, u32[]{:S(2)}, u32[]{:S(2)}) %collective-permute-start.7) | collective-permute-done | bytes 1048608 | tf_op jit(solution)/shard_map/ppermute | solution.py:14
  71.2 272.4 %while.10 = (s32[]{:T(128)}, f32[8,4,128,128]{3,2,1,0:T(8,128)S(1)}, s32[8,4,3,128]{3,1,0,2:T(4,128)S(1)}, s32[8,4,32]{2,1,0:T(4,128)S(1)}, s32[160,3,128]{2,1,0...) while((s32[]{:T(128)}, ...), condition=%wide.region_1.2_spmd, body=%wide.region_0.1_spmd.sunk | while | flops 589497728 | bytes 68511408 | solution.py:78
  72.1 11.8 %subtract_convert_fusion.2 = f32[4,32,3,128,128]{4,3,1,0,2:T(8,128)} fusion(s32[4,32,3,128]{3,1,0,2:T(8,128)S(1)} %copy.35, s32[4,3,128]{2,0,1:T(4,128)S(1)} %dynamic-slice_bitcast_fusion.2), kind=kLoop, calls=%fused_computation.2.clone.1 | loop fusion | flops 12582912 | bytes 25368576 | tf_op jit(solution)/shard_map/while/body/eval_jaxpr/convert_element_type | solution.py:26
  84.0 5.6 gather_fusion
  90.2 15.0 %fusion.56 = f32[8,4,128,128]{3,2,1,0:T(8,128)S(1)} fusion(f32[8,4,128,128]{3,2,1,0:T(8,128)S(1)} %get-tuple-element.145, s32[]{:T(128)} %get-tuple-element.144, bf16[4,32,128,128]{3,2,1,0:T(8,128)(2,1)} %bitcast.145, f32[4,32,3,128,128]{4,3,1,0,2:T(8,128)} %subtract_convert_fusion.2, f32[]{:T(128)} %bitcast.142, f32[]{:T(128)} %bitcast.143, ...), kind=kOutput, calls=%fused_computation.23.clone.1 | convolution fusion | flops 576913408 | bytes 29753360 | tf_op jit(solution)/shard_map/while/body/eval_jaxpr/gnab,gnbc->gac/dot_general | solution.py:73
  106.2 11.8 %subtract_convert_fusion.2 = f32[4,32,3,128,128]{4,3,1,0,2:T(8,128)} fusion(s32[4,32,3,128]{3,1,0,2:T(8,128)S(1)} %copy.35, s32[4,3,128]{2,0,1:T(4,128)S(1)} %dynamic-slice_bitcast_fusion.2), kind=kLoop, calls=%fused_computation.2.clone.1 | loop fusion | flops 12582912 | bytes 25368576 | tf_op jit(solution)/shard_map/while/body/eval_jaxpr/convert_element_type | solution.py:26
  118.0 5.6 gather_fusion
  124.2 15.0 %fusion.56 = f32[8,4,128,128]{3,2,1,0:T(8,128)S(1)} fusion(f32[8,4,128,128]{3,2,1,0:T(8,128)S(1)} %get-tuple-element.145, s32[]{:T(128)} %get-tuple-element.144, bf16[4,32,128,128]{3,2,1,0:T(8,128)(2,1)} %bitcast.145, f32[4,32,3,128,128]{4,3,1,0,2:T(8,128)} %subtract_convert_fusion.2, f32[]{:T(128)} %bitcast.142, f32[]{:T(128)} %bitcast.143, ...), kind=kOutput, calls=%fused_computation.23.clone.1 | convolution fusion | flops 576913408 | bytes 29753360 | tf_op jit(solution)/shard_map/while/body/eval_jaxpr/gnab,gnbc->gac/dot_general | solution.py:73
  140.2 11.8 %subtract_convert_fusion.2 = f32[4,32,3,128,128]{4,3,1,0,2:T(8,128)} fusion(s32[4,32,3,128]{3,1,0,2:T(8,128)S(1)} %copy.35, s32[4,3,128]{2,0,1:T(4,128)S(1)} %dynamic-slice_bitcast_fusion.2), kind=kLoop, calls=%fused_computation.2.clone.1 | loop fusion | flops 12582912 | bytes 25368576 | tf_op jit(solution)/shard_map/while/body/eval_jaxpr/convert_element_type | solution.py:26
  152.0 5.6 gather_fusion
  158.3 15.0 %fusion.56 = f32[8,4,128,128]{3,2,1,0:T(8,128)S(1)} fusion(f32[8,4,128,128]{3,2,1,0:T(8,128)S(1)} %get-tuple-element.145, s32[]{:T(128)} %get-tuple-element.144, bf16[4,32,128,128]{3,2,1,0:T(8,128)(2,1)} %bitcast.145, f32[4,32,3,128,128]{4,3,1,0,2:T(8,128)} %subtract_convert_fusion.2, f32[]{:T(128)} %bitcast.142, f32[]{:T(128)} %bitcast.143, ...), kind=kOutput, calls=%fused_computation.23.clone.1 | convolution fusion | flops 576913408 | bytes 29753360 | tf_op jit(solution)/shard_map/while/body/eval_jaxpr/gnab,gnbc->gac/dot_general | solution.py:73
  174.2 11.8 %subtract_convert_fusion.2 = f32[4,32,3,128,128]{4,3,1,0,2:T(8,128)} fusion(s32[4,32,3,128]{3,1,0,2:T(8,128)S(1)} %copy.35, s32[4,3,128]{2,0,1:T(4,128)S(1)} %dynamic-slice_bitcast_fusion.2), kind=kLoop, calls=%fused_computation.2.clone.1 | loop fusion | flops 12582912 | bytes 25368576 | tf_op jit(solution)/shard_map/while/body/eval_jaxpr/convert_element_type | solution.py:26
  186.0 5.6 gather_fusion
  192.3 15.0 %fusion.56 = f32[8,4,128,128]{3,2,1,0:T(8,128)S(1)} fusion(f32[8,4,128,128]{3,2,1,0:T(8,128)S(1)} %get-tuple-element.145, s32[]{:T(128)} %get-tuple-element.144, bf16[4,32,128,128]{3,2,1,0:T(8,128)(2,1)} %bitcast.145, f32[4,32,3,128,128]{4,3,1,0,2:T(8,128)} %subtract_convert_fusion.2, f32[]{:T(128)} %bitcast.142, f32[]{:T(128)} %bitcast.143, ...), kind=kOutput, calls=%fused_computation.23.clone.1 | convolution fusion | flops 576913408 | bytes 29753360 | tf_op jit(solution)/shard_map/while/body/eval_jaxpr/gnab,gnbc->gac/dot_general | solution.py:73
  208.2 11.8 %subtract_convert_fusion.2 = f32[4,32,3,128,128]{4,3,1,0,2:T(8,128)} fusion(s32[4,32,3,128]{3,1,0,2:T(8,128)S(1)} %copy.35, s32[4,3,128]{2,0,1:T(4,128)S(1)} %dynamic-slice_bitcast_fusion.2), kind=kLoop, calls=%fused_computation.2.clone.1 | loop fusion | flops 12582912 | bytes 25368576 | tf_op jit(solution)/shard_map/while/body/eval_jaxpr/convert_element_type | solution.py:26
  220.1 5.6 gather_fusion
  226.3 15.0 %fusion.56 = f32[8,4,128,128]{3,2,1,0:T(8,128)S(1)} fusion(f32[8,4,128,128]{3,2,1,0:T(8,128)S(1)} %get-tuple-element.145, s32[]{:T(128)} %get-tuple-element.144, bf16[4,32,128,128]{3,2,1,0:T(8,128)(2,1)} %bitcast.145, f32[4,32,3,128,128]{4,3,1,0,2:T(8,128)} %subtract_convert_fusion.2, f32[]{:T(128)} %bitcast.142, f32[]{:T(128)} %bitcast.143, ...), kind=kOutput, calls=%fused_computation.23.clone.1 | convolution fusion | flops 576913408 | bytes 29753360 | tf_op jit(solution)/shard_map/while/body/eval_jaxpr/gnab,gnbc->gac/dot_general | solution.py:73
  242.3 11.8 %subtract_convert_fusion.2 = f32[4,32,3,128,128]{4,3,1,0,2:T(8,128)} fusion(s32[4,32,3,128]{3,1,0,2:T(8,128)S(1)} %copy.35, s32[4,3,128]{2,0,1:T(4,128)S(1)} %dynamic-slice_bitcast_fusion.2), kind=kLoop, calls=%fused_computation.2.clone.1 | loop fusion | flops 12582912 | bytes 25368576 | tf_op jit(solution)/shard_map/while/body/eval_jaxpr/convert_element_type | solution.py:26
  254.1 5.6 gather_fusion
  260.3 15.0 %fusion.56 = f32[8,4,128,128]{3,2,1,0:T(8,128)S(1)} fusion(f32[8,4,128,128]{3,2,1,0:T(8,128)S(1)} %get-tuple-element.145, s32[]{:T(128)} %get-tuple-element.144, bf16[4,32,128,128]{3,2,1,0:T(8,128)(2,1)} %bitcast.145, f32[4,32,3,128,128]{4,3,1,0,2:T(8,128)} %subtract_convert_fusion.2, f32[]{:T(128)} %bitcast.142, f32[]{:T(128)} %bitcast.143, ...), kind=kOutput, calls=%fused_computation.23.clone.1 | convolution fusion | flops 576913408 | bytes 29753360 | tf_op jit(solution)/shard_map/while/body/eval_jaxpr/gnab,gnbc->gac/dot_general | solution.py:73
  276.3 11.8 %subtract_convert_fusion.2 = f32[4,32,3,128,128]{4,3,1,0,2:T(8,128)} fusion(s32[4,32,3,128]{3,1,0,2:T(8,128)S(1)} %copy.35, s32[4,3,128]{2,0,1:T(4,128)S(1)} %dynamic-slice_bitcast_fusion.2), kind=kLoop, calls=%fused_computation.2.clone.1 | loop fusion | flops 12582912 | bytes 25368576 | tf_op jit(solution)/shard_map/while/body/eval_jaxpr/convert_element_type | solution.py:26
  288.1 5.6 gather_fusion
  294.4 15.0 %fusion.56 = f32[8,4,128,128]{3,2,1,0:T(8,128)S(1)} fusion(f32[8,4,128,128]{3,2,1,0:T(8,128)S(1)} %get-tuple-element.145, s32[]{:T(128)} %get-tuple-element.144, bf16[4,32,128,128]{3,2,1,0:T(8,128)(2,1)} %bitcast.145, f32[4,32,3,128,128]{4,3,1,0,2:T(8,128)} %subtract_convert_fusion.2, f32[]{:T(128)} %bitcast.142, f32[]{:T(128)} %bitcast.143, ...), kind=kOutput, calls=%fused_computation.23.clone.1 | convolution fusion | flops 576913408 | bytes 29753360 | tf_op jit(solution)/shard_map/while/body/eval_jaxpr/gnab,gnbc->gac/dot_general | solution.py:73
  310.3 11.8 %subtract_convert_fusion.2 = f32[4,32,3,128,128]{4,3,1,0,2:T(8,128)} fusion(s32[4,32,3,128]{3,1,0,2:T(8,128)S(1)} %copy.35, s32[4,3,128]{2,0,1:T(4,128)S(1)} %dynamic-slice_bitcast_fusion.2), kind=kLoop, calls=%fused_computation.2.clone.1 | loop fusion | flops 12582912 | bytes 25368576 | tf_op jit(solution)/shard_map/while/body/eval_jaxpr/convert_element_type | solution.py:26
  322.1 5.6 gather_fusion
  328.4 15.0 %fusion.56 = f32[8,4,128,128]{3,2,1,0:T(8,128)S(1)} fusion(f32[8,4,128,128]{3,2,1,0:T(8,128)S(1)} %get-tuple-element.145, s32[]{:T(128)} %get-tuple-element.144, bf16[4,32,128,128]{3,2,1,0:T(8,128)(2,1)} %bitcast.145, f32[4,32,3,128,128]{4,3,1,0,2:T(8,128)} %subtract_convert_fusion.2, f32[]{:T(128)} %bitcast.142, f32[]{:T(128)} %bitcast.143, ...), kind=kOutput, calls=%fused_computation.23.clone.1 | convolution fusion | flops 576913408 | bytes 29753360 | tf_op jit(solution)/shard_map/while/body/eval_jaxpr/gnab,gnbc->gac/dot_general | solution.py:73
  347.8 242.3 %all-reduce.2.cloned.1.call-done = f32[128,128]{0,1:T(8,128)} async-done(((f32[128,128]{0,1:T(8,128)}), f32[128,128]{0,1:T(8,128)}) %all-reduce.2.cloned.1.call-update) | async-done | bytes 65552 | tf_op jit(solution)/shard_map/psum | solution.py:92
  591.8 11.7 %cholesky.17 = f32[128,128]{1,0:T(8,128)S(1)} custom-call(f32[128,128]{1,0:T(8,128)S(1)} %fusion.33), custom_call_target="Cholesky" | custom-call | tf_op jit(solution)/shard_map/jit(cholesky)/cholesky | solution.py:92
  604.9 9.8 %custom-call.7 = f32[1,128,128]{1,2,0:T(8,128)S(1)} custom-call(f32[1,128,128]{2,1,0:T(8,128)S(1)} %get-tuple-element.79), custom_call_target="InvertDiagBlocksLowerTriangular" | custom-call | tf_op jit(solution)/shard_map/jit(_solve_triangular)/triangular_solve | solution.py:93
  (114 shorter events, 48.8 us)
Async XLA Ops:
  7.2 50.2 %copy-start.1 = (bf16[4096,128]{1,0:T(8,128)(2,1)S(1)}, bf16[4096,128]{1,0:T(8,128)(2,1)}, u32[]{:S(2)}) copy-start(bf16[4096,128]{1,0:T(8,128)(2,1)} %param.6) | copy-start | bytes 3145732
  7.2 582.9 %all-reduce.2.cloned.1.call-start = ((), (), s32[]{:S(2)}) async-start(), calls=%async_computation | async-start | bytes 131072 | tf_op jit(solution)/shard_map/psum | solution.py:92
  7.2 32.9 %collective-permute-start.4 = (bf16[32,128,128]{2,1,0:T(8,128)(2,1)}, bf16[32,128,128]{2,1,0:T(8,128)(2,1)}, u32[]{:S(2)}, u32[]{:S(2)}) collective-permute-start(bf16[32,128,128]{2,1,0:T(8,128)(2,1)} %bitcast.148), channel_id=1, source_target_pairs={{240,0},{0,16},{16,32},{32,48},{48,64},{64,80},{80,96},{96,112},{1... | collective-permute-start | bytes 3145736 | tf_op jit(solution)/shard_map/ppermute | solution.py:14
  11.4 29.8 %collective-permute-start.6 = (bf16[32,128,128]{2,1,0:T(8,128)(2,1)}, bf16[32,128,128]{2,1,0:T(8,128)(2,1)}, u32[]{:S(2)}, u32[]{:S(2)}) collective-permute-start(bf16[32,128,128]{2,1,0:T(8,128)(2,1)} %bitcast.149), channel_id=1, source_target_pairs={{16,0},{32,16},{48,32},{64,48},{80,64},{96,80},{112,96},{128,112},... | collective-permute-start | bytes 3145736 | tf_op jit(solution)/shard_map/ppermute | solution.py:14
  11.4 20.0 %collective-permute-start = (s32[3,4096]{1,0:T(4,128)}, s32[3,4096]{1,0:T(4,128)S(1)}, u32[]{:S(2)}, u32[]{:S(2)}) collective-permute-start(s32[3,4096]{1,0:T(4,128)} %param.7), channel_id=1, source_target_pairs={{240,0},{0,16},{16,32},{32,48},{48,64},{64,80},{80,96},{96,112},{1... | collective-permute-start | bytes 147464 | tf_op jit(solution)/shard_map/ppermute | solution.py:14
  14.7 23.3 %collective-permute-start.2 = (s32[3,4096]{1,0:T(4,128)}, s32[3,4096]{1,0:T(4,128)S(1)}, u32[]{:S(2)}, u32[]{:S(2)}) collective-permute-start(s32[3,4096]{1,0:T(4,128)} %param.7), channel_id=1, source_target_pairs={{16,0},{32,16},{48,32},{64,48},{80,64},{96,80},{112,96},{128,112},... | collective-permute-start | bytes 147464 | tf_op jit(solution)/shard_map/ppermute | solution.py:14
  31.4 9.8 %collective-permute-start.1 = (s32[3,4096]{1,0:T(4,128)S(1)}, s32[3,4096]{1,0:T(4,128)S(1)}, u32[]{:S(2)}, u32[]{:S(2)}) collective-permute-start(s32[3,4096]{1,0:T(4,128)S(1)} %collective-permute-done), channel_id=1, source_target_pairs={{240,0},{0,16},{16,32},{32,48},{48,64},{64,80},{80,96},{96,112},{1... | collective-permute-start | bytes 147464 | tf_op jit(solution)/shard_map/ppermute | solution.py:14
  38.0 9.7 %collective-permute-start.3 = (s32[3,4096]{1,0:T(4,128)S(1)}, s32[3,4096]{1,0:T(4,128)S(1)}, u32[]{:S(2)}, u32[]{:S(2)}) collective-permute-start(s32[3,4096]{1,0:T(4,128)S(1)} %collective-permute-done.2), channel_id=1, source_target_pairs={{16,0},{32,16},{48,32},{64,48},{80,64},{96,80},{112,96},{128,112},... | collective-permute-start | bytes 147464 | tf_op jit(solution)/shard_map/ppermute | solution.py:14
  40.1 15.8 %collective-permute-start.5 = (bf16[32,128,128]{2,1,0:T(8,128)(2,1)}, bf16[32,128,128]{2,1,0:T(8,128)(2,1)S(1)}, u32[]{:S(2)}, u32[]{:S(2)}) collective-permute-start(bf16[32,128,128]{2,1,0:T(8,128)(2,1)} %collective-permute-done.4), channel_id=1, source_target_pairs={{240,0},{0,16},{16,32},{32,48},{48,64},{64,80},{80,96},{96,112},{1... | collective-permute-start | bytes 3145736 | tf_op jit(solution)/shard_map/ppermute | solution.py:14
  41.3 27.4 %collective-permute-start.7 = (bf16[32,128,128]{2,1,0:T(8,128)(2,1)}, bf16[32,128,128]{2,1,0:T(8,128)(2,1)S(1)}, u32[]{:S(2)}, u32[]{:S(2)}) collective-permute-start(bf16[32,128,128]{2,1,0:T(8,128)(2,1)} %collective-permute-done.6), channel_id=1, source_target_pairs={{16,0},{32,16},{48,32},{64,48},{80,64},{96,80},{112,96},{128,112},... | collective-permute-start | bytes 3145736 | tf_op jit(solution)/shard_map/ppermute | solution.py:14
  47.9 23.4 %copy-start.3 = (f32[3]{0:T(128)S(1)}, f32[3]{0:T(128)}, u32[]{:S(2)}) copy-start(f32[3]{0:T(128)} %param.9) | copy-start | bytes 40
  68.8 2.4 copy-start
  84.0 6.3 %copy-start.2 = (bf16[4096,128]{1,0:T(8,128)(2,1)S(1)}, bf16[4096,128]{1,0:T(8,128)(2,1)}, u32[]{:S(2)}) copy-start(bf16[4096,128]{1,0:T(8,128)(2,1)} %get-tuple-element.174) | copy-start | bytes 3145732 | tf_op jit(solution)/shard_map/while
  118.0 6.3 %copy-start.2 = (bf16[4096,128]{1,0:T(8,128)(2,1)S(1)}, bf16[4096,128]{1,0:T(8,128)(2,1)}, u32[]{:S(2)}) copy-start(bf16[4096,128]{1,0:T(8,128)(2,1)} %get-tuple-element.174) | copy-start | bytes 3145732 | tf_op jit(solution)/shard_map/while
  152.0 6.3 %copy-start.2 = (bf16[4096,128]{1,0:T(8,128)(2,1)S(1)}, bf16[4096,128]{1,0:T(8,128)(2,1)}, u32[]{:S(2)}) copy-start(bf16[4096,128]{1,0:T(8,128)(2,1)} %get-tuple-element.174) | copy-start | bytes 3145732 | tf_op jit(solution)/shard_map/while
  186.0 6.3 %copy-start.2 = (bf16[4096,128]{1,0:T(8,128)(2,1)S(1)}, bf16[4096,128]{1,0:T(8,128)(2,1)}, u32[]{:S(2)}) copy-start(bf16[4096,128]{1,0:T(8,128)(2,1)} %get-tuple-element.174) | copy-start | bytes 3145732 | tf_op jit(solution)/shard_map/while
  220.1 6.3 %copy-start.2 = (bf16[4096,128]{1,0:T(8,128)(2,1)S(1)}, bf16[4096,128]{1,0:T(8,128)(2,1)}, u32[]{:S(2)}) copy-start(bf16[4096,128]{1,0:T(8,128)(2,1)} %get-tuple-element.174) | copy-start | bytes 3145732 | tf_op jit(solution)/shard_map/while
  254.1 6.3 %copy-start.2 = (bf16[4096,128]{1,0:T(8,128)(2,1)S(1)}, bf16[4096,128]{1,0:T(8,128)(2,1)}, u32[]{:S(2)}) copy-start(bf16[4096,128]{1,0:T(8,128)(2,1)} %get-tuple-element.174) | copy-start | bytes 3145732 | tf_op jit(solution)/shard_map/while
  288.1 6.3 %copy-start.2 = (bf16[4096,128]{1,0:T(8,128)(2,1)S(1)}, bf16[4096,128]{1,0:T(8,128)(2,1)}, u32[]{:S(2)}) copy-start(bf16[4096,128]{1,0:T(8,128)(2,1)} %get-tuple-element.174) | copy-start | bytes 3145732 | tf_op jit(solution)/shard_map/while
  322.1 6.3 %copy-start.2 = (bf16[4096,128]{1,0:T(8,128)(2,1)S(1)}, bf16[4096,128]{1,0:T(8,128)(2,1)}, u32[]{:S(2)}) copy-start(bf16[4096,128]{1,0:T(8,128)(2,1)} %get-tuple-element.174) | copy-start | bytes 3145732 | tf_op jit(solution)/shard_map/while
Sparse Core Ops, SparseCore 0:
  347.9 242.1 all-reduce.1
where the time goes:
time: 626 us
  waiting for transfers between devices  278 us (44%)
  matrix products  128 us (20%)
  other arithmetic  119 us (19%)
  local copies, waits for them, and re-layouts  65.2 us (10%)
  starting transfers between devices  21.4 us (3%)
  between operations  14.2 us (2%)
    psum x1, waiting for transfers between devices, on_device(): lower = jnp.linalg.cholesky(lax.psum(local_gram, ('sector', 'depth')))  242 us
    dot_general x8, matrix products, one_group(): jnp.einsum('gnab,gnbc->gac', kernel, wide_panel[rows_list], preferred_ele...  120 us
    convert_element_type x8, other arithmetic, cov_blocks(): (home[:, None, :, :, None] - remote[:, :, :, None, :]).astype(jnp.float32)  94.5 us
    gather x8, local copies, waits for them, and re-layouts, one_group(): wide_panel[rows_list]  44.8 us
    ppermute x8, waiting for transfers between devices, passed_along(): return lax.ppermute(block, axis, route)  35.2 us
    ppermute x8, starting transfers between devices, passed_along(): return lax.ppermute(block, axis, route)  21.3 us
  transfers between devices with their start and end apart: 9, of which 5 were waited for; matrix products, arithmetic and copies ran while one was open for 1% of the time, Pallas kernels for 0%

commit v1 on v0

--- a/solution.py
+++ b/solution.py
@@ -2,10 +2,14 @@
 import jax.numpy as jnp
 from jax import lax
 from jax.sharding import PartitionSpec as P
+from jax.lax import all_gather
 
 AZ_SEC = 8
 CUTOFF = 3.0
 NUGGET = 0.5
+reach_the_views = lambda incoming_x, along_axis: all_gather(incoming_x, axis_name=along_axis).sum(
+    axis=0
+)
 
 
 def passed_along(block, axis, distance):
@@ -89,7 +93,7 @@
         jnp.dot(image.T, image, precision=lax.Precision.HIGHEST, preferred_element_type=jnp.float32)
         / total_cells
     )
-    lower = jnp.linalg.cholesky(lax.psum(local_gram, ("sector", "depth")))
+    lower = jnp.linalg.cholesky(reach_the_views(local_gram, ("sector", "depth")))
     inverse = jax.scipy.linalg.solve_triangular(
         lower, jnp.eye(width, dtype=jnp.float32), lower=True
     )

time: 626 us -> 1130 us (1.81)
  waiting for transfers between devices: 278 us -> 771 us
    all_gather x0 -> x1, waiting for transfers between devices: none -> 736 us  [all_gather(incoming_x, axis_name=along_axis).sum(axis=0)]
    psum x1 -> x0, waiting for transfers between devices: 242 us -> none  [on_device(): lower = jnp.linalg.cholesky(lax.psum(local_gram, ('sector', 'depth')))]
  transfers between devices with their start and end apart: 9 -> 9, of which waited for: 5 -> 5; matrix products, arithmetic and copies ran while one was open for 1% -> 0% of each run, Pallas kernels for 0% -> 0%
where the time goes in v1:
time: 1130 us
  waiting for transfers between devices  771 us (68%)
  matrix products  132 us (12%)
  other arithmetic  125 us (11%)
  local copies, waits for them, and re-layouts  63.7 us (6%)
  starting transfers between devices  21.4 us (2%)
  between operations  14.2 us (1%)
    all_gather x1, waiting for transfers between devices, all_gather(incoming_x, axis_name=along_axis).sum(axis=0)  736 us
    dot_general x8, matrix products, one_group(): jnp.einsum('gnab,gnbc->gac', kernel, wide_panel[rows_list], preferred_ele...  124 us
    convert_element_type x8, other arithmetic, cov_blocks(): (home[:, None, :, :, None] - remote[:, :, :, None, :]).astype(jnp.float32)  94.5 us
    gather x8, local copies, waits for them, and re-layouts, one_group(): wide_panel[rows_list]  44.1 us
    ppermute x8, waiting for transfers between devices, passed_along(): return lax.ppermute(block, axis, route)  35.2 us
  transfers between devices with their start and end apart: 9, of which 5 were waited for; matrix products, arithmetic and copies ran while one was open for 0% of the time, Pallas kernels for 0%

profile of v1, /device:TPU:1, one launch (start us, length us, event | category | flops | bytes accessed | tf_op | source)
XLA Modules:
  0.0 1127.4 jit_solution(10961353376852539779)
XLA Ops:
  15.9 15.5 %collective-permute-done = s32[3,4096]{1,0:T(4,128)S(1)} collective-permute-done((s32[3,4096]{1,0:T(4,128)}, s32[3,4096]{1,0:T(4,128)S(1)}, u32[]{:S(2)}, u32[]{:S(2)}) %collective-permute-start) | collective-permute-done | bytes 49184 | tf_op jit(solution)/shard_map/ppermute | solution.py:18
  41.3 5.5 collective-permute-start.7
  47.9 8.0 collective-permute-done.5
  58.9 9.8 collective-permute-done.7
  71.2 275.9 %while.10 = (s32[]{:T(128)}, f32[8,4,128,128]{3,2,1,0:T(8,128)S(1)}, s32[8,4,3,128]{3,1,0,2:T(4,128)S(1)}, s32[8,4,32]{2,1,0:T(4,128)S(1)}, s32[160,3,128]{2,1,0...) while((s32[]{:T(128)}, ...), condition=%wide.region_1.2_spmd, body=%wide.region_0.1_spmd.sunk | while | flops 589497728 | bytes 64317068 | solution.py:82
  72.1 11.8 %subtract_convert_fusion.2 = f32[4,32,3,128,128]{4,3,1,0,2:T(8,128)} fusion(s32[4,32,3,128]{3,1,0,2:T(8,128)S(1)} %copy.38, s32[4,3,128]{2,0,1:T(4,128)S(1)} %dynamic-slice_bitcast_fusion.2), kind=kLoop, calls=%fused_computation.2.clone.1 | loop fusion | flops 12582912 | bytes 25368576 | tf_op jit(solution)/shard_map/while/body/eval_jaxpr/convert_element_type | solution.py:30
  83.9 5.5 gather_fusion
  90.1 15.5 %fusion.56 = f32[8,4,128,128]{3,2,1,0:T(8,128)S(1)} fusion(f32[8,4,128,128]{3,2,1,0:T(8,128)S(1)} %get-tuple-element.155, s32[]{:T(128)} %get-tuple-element.154, bf16[4,32,128,128]{3,2,1,0:T(8,128)(2,1)} %bitcast.148, f32[4,32,3,128,128]{4,3,1,0,2:T(8,128)} %subtract_convert_fusion.2, f32[]{:T(128)} %bitcast.145, f32[]{:T(128)} %bitcast.146, ...), kind=kOutput, calls=%fused_computation.23.clone.1 | convolution fusion | flops 576913408 | bytes 29753360 | tf_op jit(solution)/shard_map/while/body/eval_jaxpr/gnab,gnbc->gac/dot_general | solution.py:77
  106.6 11.8 %subtract_convert_fusion.2 = f32[4,32,3,128,128]{4,3,1,0,2:T(8,128)} fusion(s32[4,32,3,128]{3,1,0,2:T(8,128)S(1)} %copy.38, s32[4,3,128]{2,0,1:T(4,128)S(1)} %dynamic-slice_bitcast_fusion.2), kind=kLoop, calls=%fused_computation.2.clone.1 | loop fusion | flops 12582912 | bytes 25368576 | tf_op jit(solution)/shard_map/while/body/eval_jaxpr/convert_element_type | solution.py:30
  118.4 5.5 gather_fusion
  124.6 15.5 %fusion.56 = f32[8,4,128,128]{3,2,1,0:T(8,128)S(1)} fusion(f32[8,4,128,128]{3,2,1,0:T(8,128)S(1)} %get-tuple-element.155, s32[]{:T(128)} %get-tuple-element.154, bf16[4,32,128,128]{3,2,1,0:T(8,128)(2,1)} %bitcast.148, f32[4,32,3,128,128]{4,3,1,0,2:T(8,128)} %subtract_convert_fusion.2, f32[]{:T(128)} %bitcast.145, f32[]{:T(128)} %bitcast.146, ...), kind=kOutput, calls=%fused_computation.23.clone.1 | convolution fusion | flops 576913408 | bytes 29753360 | tf_op jit(solution)/shard_map/while/body/eval_jaxpr/gnab,gnbc->gac/dot_general | solution.py:77
  141.1 11.8 %subtract_convert_fusion.2 = f32[4,32,3,128,128]{4,3,1,0,2:T(8,128)} fusion(s32[4,32,3,128]{3,1,0,2:T(8,128)S(1)} %copy.38, s32[4,3,128]{2,0,1:T(4,128)S(1)} %dynamic-slice_bitcast_fusion.2), kind=kLoop, calls=%fused_computation.2.clone.1 | loop fusion | flops 12582912 | bytes 25368576 | tf_op jit(solution)/shard_map/while/body/eval_jaxpr/convert_element_type | solution.py:30
  152.9 5.5 gather_fusion
  159.1 15.5 %fusion.56 = f32[8,4,128,128]{3,2,1,0:T(8,128)S(1)} fusion(f32[8,4,128,128]{3,2,1,0:T(8,128)S(1)} %get-tuple-element.155, s32[]{:T(128)} %get-tuple-element.154, bf16[4,32,128,128]{3,2,1,0:T(8,128)(2,1)} %bitcast.148, f32[4,32,3,128,128]{4,3,1,0,2:T(8,128)} %subtract_convert_fusion.2, f32[]{:T(128)} %bitcast.145, f32[]{:T(128)} %bitcast.146, ...), kind=kOutput, calls=%fused_computation.23.clone.1 | convolution fusion | flops 576913408 | bytes 29753360 | tf_op jit(solution)/shard_map/while/body/eval_jaxpr/gnab,gnbc->gac/dot_general | solution.py:77
  175.5 11.8 %subtract_convert_fusion.2 = f32[4,32,3,128,128]{4,3,1,0,2:T(8,128)} fusion(s32[4,32,3,128]{3,1,0,2:T(8,128)S(1)} %copy.38, s32[4,3,128]{2,0,1:T(4,128)S(1)} %dynamic-slice_bitcast_fusion.2), kind=kLoop, calls=%fused_computation.2.clone.1 | loop fusion | flops 12582912 | bytes 25368576 | tf_op jit(solution)/shard_map/while/body/eval_jaxpr/convert_element_type | solution.py:30
  187.3 5.5 gather_fusion
  193.5 15.5 %fusion.56 = f32[8,4,128,128]{3,2,1,0:T(8,128)S(1)} fusion(f32[8,4,128,128]{3,2,1,0:T(8,128)S(1)} %get-tuple-element.155, s32[]{:T(128)} %get-tuple-element.154, bf16[4,32,128,128]{3,2,1,0:T(8,128)(2,1)} %bitcast.148, f32[4,32,3,128,128]{4,3,1,0,2:T(8,128)} %subtract_convert_fusion.2, f32[]{:T(128)} %bitcast.145, f32[]{:T(128)} %bitcast.146, ...), kind=kOutput, calls=%fused_computation.23.clone.1 | convolution fusion | flops 576913408 | bytes 29753360 | tf_op jit(solution)/shard_map/while/body/eval_jaxpr/gnab,gnbc->gac/dot_general | solution.py:77
  210.0 11.8 %subtract_convert_fusion.2 = f32[4,32,3,128,128]{4,3,1,0,2:T(8,128)} fusion(s32[4,32,3,128]{3,1,0,2:T(8,128)S(1)} %copy.38, s32[4,3,128]{2,0,1:T(4,128)S(1)} %dynamic-slice_bitcast_fusion.2), kind=kLoop, calls=%fused_computation.2.clone.1 | loop fusion | flops 12582912 | bytes 25368576 | tf_op jit(solution)/shard_map/while/body/eval_jaxpr/convert_element_type | solution.py:30
  221.8 5.5 gather_fusion
  228.0 15.5 %fusion.56 = f32[8,4,128,128]{3,2,1,0:T(8,128)S(1)} fusion(f32[8,4,128,128]{3,2,1,0:T(8,128)S(1)} %get-tuple-element.155, s32[]{:T(128)} %get-tuple-element.154, bf16[4,32,128,128]{3,2,1,0:T(8,128)(2,1)} %bitcast.148, f32[4,32,3,128,128]{4,3,1,0,2:T(8,128)} %subtract_convert_fusion.2, f32[]{:T(128)} %bitcast.145, f32[]{:T(128)} %bitcast.146, ...), kind=kOutput, calls=%fused_computation.23.clone.1 | convolution fusion | flops 576913408 | bytes 29753360 | tf_op jit(solution)/shard_map/while/body/eval_jaxpr/gnab,gnbc->gac/dot_general | solution.py:77
  244.5 11.8 %subtract_convert_fusion.2 = f32[4,32,3,128,128]{4,3,1,0,2:T(8,128)} fusion(s32[4,32,3,128]{3,1,0,2:T(8,128)S(1)} %copy.38, s32[4,3,128]{2,0,1:T(4,128)S(1)} %dynamic-slice_bitcast_fusion.2), kind=kLoop, calls=%fused_computation.2.clone.1 | loop fusion | flops 12582912 | bytes 25368576 | tf_op jit(solution)/shard_map/while/body/eval_jaxpr/convert_element_type | solution.py:30
  262.4 15.5 %fusion.56 = f32[8,4,128,128]{3,2,1,0:T(8,128)S(1)} fusion(f32[8,4,128,128]{3,2,1,0:T(8,128)S(1)} %get-tuple-element.155, s32[]{:T(128)} %get-tuple-element.154, bf16[4,32,128,128]{3,2,1,0:T(8,128)(2,1)} %bitcast.148, f32[4,32,3,128,128]{4,3,1,0,2:T(8,128)} %subtract_convert_fusion.2, f32[]{:T(128)} %bitcast.145, f32[]{:T(128)} %bitcast.146, ...), kind=kOutput, calls=%fused_computation.23.clone.1 | convolution fusion | flops 576913408 | bytes 29753360 | tf_op jit(solution)/shard_map/while/body/eval_jaxpr/gnab,gnbc->gac/dot_general | solution.py:77
  278.9 11.8 %subtract_convert_fusion.2 = f32[4,32,3,128,128]{4,3,1,0,2:T(8,128)} fusion(s32[4,32,3,128]{3,1,0,2:T(8,128)S(1)} %copy.38, s32[4,3,128]{2,0,1:T(4,128)S(1)} %dynamic-slice_bitcast_fusion.2), kind=kLoop, calls=%fused_computation.2.clone.1 | loop fusion | flops 12582912 | bytes 25368576 | tf_op jit(solution)/shard_map/while/body/eval_jaxpr/convert_element_type | solution.py:30
  290.7 5.5 gather_fusion
  296.9 15.5 %fusion.56 = f32[8,4,128,128]{3,2,1,0:T(8,128)S(1)} fusion(f32[8,4,128,128]{3,2,1,0:T(8,128)S(1)} %get-tuple-element.155, s32[]{:T(128)} %get-tuple-element.154, bf16[4,32,128,128]{3,2,1,0:T(8,128)(2,1)} %bitcast.148, f32[4,32,3,128,128]{4,3,1,0,2:T(8,128)} %subtract_convert_fusion.2, f32[]{:T(128)} %bitcast.145, f32[]{:T(128)} %bitcast.146, ...), kind=kOutput, calls=%fused_computation.23.clone.1 | convolution fusion | flops 576913408 | bytes 29753360 | tf_op jit(solution)/shard_map/while/body/eval_jaxpr/gnab,gnbc->gac/dot_general | solution.py:77
  313.4 11.8 %subtract_convert_fusion.2 = f32[4,32,3,128,128]{4,3,1,0,2:T(8,128)} fusion(s32[4,32,3,128]{3,1,0,2:T(8,128)S(1)} %copy.38, s32[4,3,128]{2,0,1:T(4,128)S(1)} %dynamic-slice_bitcast_fusion.2), kind=kLoop, calls=%fused_computation.2.clone.1 | loop fusion | flops 12582912 | bytes 25368576 | tf_op jit(solution)/shard_map/while/body/eval_jaxpr/convert_element_type | solution.py:30
  325.2 5.5 gather_fusion
  331.4 15.5 %fusion.56 = f32[8,4,128,128]{3,2,1,0:T(8,128)S(1)} fusion(f32[8,4,128,128]{3,2,1,0:T(8,128)S(1)} %get-tuple-element.155, s32[]{:T(128)} %get-tuple-element.154, bf16[4,32,128,128]{3,2,1,0:T(8,128)(2,1)} %bitcast.148, f32[4,32,3,128,128]{4,3,1,0,2:T(8,128)} %subtract_convert_fusion.2, f32[]{:T(128)} %bitcast.145, f32[]{:T(128)} %bitcast.146, ...), kind=kOutput, calls=%fused_computation.23.clone.1 | convolution fusion | flops 576913408 | bytes 29753360 | tf_op jit(solution)/shard_map/while/body/eval_jaxpr/gnab,gnbc->gac/dot_general | solution.py:77
  351.3 735.6 %all-gather.3.cloned.1.call-done = f32[32768,128]{1,0:T(8,128)} async-done(((f32[128,128]{1,0:T(8,128)}), f32[32768,128]{1,0:T(8,128)}) %all-gather.3.cloned.1.call-update) | async-done | bytes 16777232 | tf_op jit(solution)/shard_map/all_gather | solution.py:10
  1086.8 6.6 reduce_sum.9
  1093.5 11.7 %cholesky.17 = f32[128,128]{1,0:T(8,128)S(1)} custom-call(f32[128,128]{1,0:T(8,128)S(1)} %fusion.33), custom_call_target="Cholesky" | custom-call | tf_op jit(solution)/shard_map/jit(cholesky)/cholesky | solution.py:96
  1106.6 9.8 custom-call.7
  (99 shorter events, 52.6 us)
Async XLA Ops:
  7.2 1079.7 %all-gather.3.cloned.1.call-start = ((), (), s32[]{:S(2)}) async-start(), calls=%async_computation | async-start | bytes 16842752 | tf_op jit(solution)/shard_map/all_gather | solution.py:10
  7.2 32.9 %collective-permute-start.4 = (bf16[32,128,128]{2,1,0:T(8,128)(2,1)}, bf16[32,128,128]{2,1,0:T(8,128)(2,1)}, u32[]{:S(2)}, u32[]{:S(2)}) collective-permute-start(bf16[32,128,128]{2,1,0:T(8,128)(2,1)} %bitcast.152), channel_id=1, source_target_pairs={{240,0},{0,16},{16,32},{32,48},{48,64},{64,80},{80,96},{96,112},{1... | collective-permute-start | bytes 3145736 | tf_op jit(solution)/shard_map/ppermute | solution.py:18
  11.4 29.8 %collective-permute-start.6 = (bf16[32,128,128]{2,1,0:T(8,128)(2,1)}, bf16[32,128,128]{2,1,0:T(8,128)(2,1)}, u32[]{:S(2)}, u32[]{:S(2)}) collective-permute-start(bf16[32,128,128]{2,1,0:T(8,128)(2,1)} %bitcast.153), channel_id=1, source_target_pairs={{16,0},{32,16},{48,32},{64,48},{80,64},{96,80},{112,96},{128,112},... | collective-permute-start | bytes 3145736 | tf_op jit(solution)/shard_map/ppermute | solution.py:18
  11.4 20.0 %collective-permute-start = (s32[3,4096]{1,0:T(4,128)}, s32[3,4096]{1,0:T(4,128)S(1)}, u32[]{:S(2)}, u32[]{:S(2)}) collective-permute-start(s32[3,4096]{1,0:T(4,128)} %param.7), channel_id=1, source_target_pairs={{240,0},{0,16},{16,32},{32,48},{48,64},{64,80},{80,96},{96,112},{1... | collective-permute-start | bytes 147464 | tf_op jit(solution)/shard_map/ppermute | solution.py:18
  14.7 23.3 %collective-permute-start.2 = (s32[3,4096]{1,0:T(4,128)}, s32[3,4096]{1,0:T(4,128)S(1)}, u32[]{:S(2)}, u32[]{:S(2)}) collective-permute-start(s32[3,4096]{1,0:T(4,128)} %param.7), channel_id=1, source_target_pairs={{16,0},{32,16},{48,32},{64,48},{80,64},{96,80},{112,96},{128,112},... | collective-permute-start | bytes 147464 | tf_op jit(solution)/shard_map/ppermute | solution.py:18
  31.4 9.8 collective-permute-start.1
  36.0 21.3 %copy-start.1 = (bf16[4096,128]{1,0:T(8,128)(2,1)S(1)}, bf16[4096,128]{1,0:T(8,128)(2,1)}, u32[]{:S(2)}) copy-start(bf16[4096,128]{1,0:T(8,128)(2,1)} %param.6) | copy-start | bytes 3145732
  38.0 9.7 collective-permute-start.3
  40.1 15.8 %collective-permute-start.5 = (bf16[32,128,128]{2,1,0:T(8,128)(2,1)}, bf16[32,128,128]{2,1,0:T(8,128)(2,1)S(1)}, u32[]{:S(2)}, u32[]{:S(2)}) collective-permute-start(bf16[32,128,128]{2,1,0:T(8,128)(2,1)} %collective-permute-done.4), channel_id=1, source_target_pairs={{240,0},{0,16},{16,32},{32,48},{48,64},{64,80},{80,96},{96,112},{1... | collective-permute-start | bytes 3145736 | tf_op jit(solution)/shard_map/ppermute | solution.py:18
  41.3 27.4 %collective-permute-start.7 = (bf16[32,128,128]{2,1,0:T(8,128)(2,1)}, bf16[32,128,128]{2,1,0:T(8,128)(2,1)S(1)}, u32[]{:S(2)}, u32[]{:S(2)}) collective-permute-start(bf16[32,128,128]{2,1,0:T(8,128)(2,1)} %collective-permute-done.6), channel_id=1, source_target_pairs={{16,0},{32,16},{48,32},{64,48},{80,64},{96,80},{112,96},{128,112},... | collective-permute-start | bytes 3145736 | tf_op jit(solution)/shard_map/ppermute | solution.py:18
  47.9 23.4 %copy-start.2 = (f32[3]{0:T(128)S(1)}, f32[3]{0:T(128)}, u32[]{:S(2)}) copy-start(f32[3]{0:T(128)} %param.9) | copy-start | bytes 40
  68.8 2.4 copy-start
Sparse Core Ops, SparseCore 0:
  351.4 735.4 all-gather.2
